TPU v7x, 32 devices: a whole 2x2x4 slice. The times are simulated.
32 devices in a mesh: grp: 2 (over y), row: 4 (over z), col: 2 (over x), sub: 2 (over core).
Axes of the slice: x: 2, y: 2, z: 4, core: 2. Of those that a mesh axis runs over, the one named last changes fastest.
Arguments:
- left_features: bfloat16 [256, 256, 128], P(('grp', 'row'), ('col', 'sub')), parts along dimension 0, may hold values from -16 to 16
- right_features: bfloat16 [256, 256, 128], P(('grp', 'row'), ('col', 'sub')), parts along dimension 0, may hold values from -16 to 16
- left_image: float32 [3, 256, 256], P(None, ('grp', 'row'), ('col', 'sub')), parts along dimension 1, may hold values from -4 to 4
- query_key: bfloat16 [128, 128], replicated, may hold values from -0.5 to 0.5
- value_weight: bfloat16 [128, 128], replicated, may hold values from -0.5 to 0.5
- out_weight: bfloat16 [128, 128], replicated, may hold values from -0.5 to 0.5
- occlusion_weight: float32 [128], replicated, may hold values from -0.5 to 0.5
- first_conv: bfloat16 [9, 64, 5], replicated, may hold values from -0.875 to 0.875
- middle_conv: bfloat16 [3, 9, 64, 64], replicated, may hold values from -0.25 to 0.25
- last_conv: bfloat16 [9, 2, 64], replicated, may hold values from -0.25 to 0.25
Outputs:
- disparity_out: float32 [256, 256], P(('grp', 'row'), ('col', 'sub')), parts along dimension 0
- occlusion_out: float32 [256, 256], P(('grp', 'row'), ('col', 'sub')), parts along dimension 0
There are 2 independent parts, one for each index of `grp`. A program takes and returns all parts, laid end to end along the dimension named above; an argument that names none is the same for every part. Nothing has to cross between parts.
All inputs are finite; a program needn't handle non-finite values.
Results may differ from a plain program's by a relative error of at most 0.0033.
Values may be sent and summed in bfloat16 or wider, within the bound.
No kernel may reach another device: no remote copies, remote signals or barrier semaphores. Data moves between devices by JAX's collectives and lax.ppermute only.
A program may use at most 64 MiB of HBM per device.

v0:
```python
import jax
import jax.numpy as jnp
from jax import lax
from jax.sharding import PartitionSpec as P

C = 128
HEADS = 8
HEAD = 16


def with_halo(cells, sides, width):
    for axis, dim in sides:
        count = lax.axis_size(axis)
        ends = count - 1
        head = lax.slice_in_dim(cells, 0, width, axis=dim)
        tail = lax.slice_in_dim(cells, cells.shape[dim] - width, cells.shape[dim], axis=dim)
        cells = jnp.concatenate(
            [
                lax.ppermute(tail, axis, [(i, (i + 1) % count) for i in range(ends)]),
                cells,
                lax.ppermute(head, axis, [((i + 1) % count, i) for i in range(ends)]),
            ],
            axis=dim,
        )
    return cells


def conv_valid(source, weight):
    height = source.shape[1] - 2
    across = source.shape[2] - 2
    summed = jnp.zeros((weight.shape[1], height, across), jnp.float32)
    for offset in range(9):
        window = source[:, offset // 3 : offset // 3 + height, offset % 3 : offset % 3 + across]
        summed = summed + jnp.einsum(
            "oc,crw->orw", weight[offset], window, preferred_element_type=jnp.float32
        )
    return summed


def layer_same(source, weight):
    padded = with_halo(source, (("row", 1), (("col", "sub"), 2)), 1)
    return conv_valid(padded, weight)


def occlusion_logit(gathered, out_weight, occlusion_weight):
    attended = jnp.einsum("rwc,cd->rwd", gathered, out_weight, preferred_element_type=jnp.float32)
    centre = jnp.mean(attended, axis=-1, keepdims=True)
    spread = jnp.mean((attended - centre) ** 2, axis=-1, keepdims=True)
    normalized = (attended - centre) * lax.rsqrt(spread + 1e-05)
    return jnp.einsum("rwc,c->rw", normalized, occlusion_weight, precision=lax.Precision.HIGHEST)


def per_device(
    left_features,
    right_features,
    left_image,
    query_key,
    value_weight,
    out_weight,
    occlusion_weight,
    first_conv,
    middle_conv,
    last_conv,
):
    tile_rows = left_features.shape[0]
    tile_cols = left_features.shape[1]
    group_size = lax.axis_size(("col", "sub"))
    row_length = tile_cols * group_size
    scaling = HEAD ** (-0.5)
    positions = jnp.arange(row_length)
    allowed = positions[None, :] <= positions[:, None]
    places = positions.astype(jnp.float32)

    def attend(inputs):
        query_block, key_block, value_block = inputs
        scores = jnp.einsum(
            "bihd,bjhd->bhij", query_block, key_block, preferred_element_type=jnp.float32
        )
        scores = jnp.where(allowed[None, None], scores, -jnp.inf)
        largest = jnp.max(scores, axis=-1, keepdims=True)
        exponent = jnp.exp(scores - largest)
        totals = jnp.sum(exponent, axis=-1, keepdims=True)
        probabilities = (exponent / totals).astype(jnp.bfloat16)
        blended = jnp.einsum(
            "bhij,bjhd->bihd", probabilities, value_block, preferred_element_type=jnp.float32
        ).astype(jnp.bfloat16)
        weighted = jnp.einsum("bhij,j->bhi", exponent, places, precision=lax.Precision.HIGHEST)
        shifts = places[None, None, :] - weighted / totals[..., 0]
        return (blended, jnp.sum(shifts, axis=1))

    band_count = tile_rows // group_size
    full_left, full_right = (
        lax.all_to_all(left_features, ("col", "sub"), split_axis=0, concat_axis=1, tiled=True),
        lax.all_to_all(right_features, ("col", "sub"), split_axis=0, concat_axis=1, tiled=True),
    )
    queries = (
        jnp.einsum("rwc,cd->rwd", full_left, query_key, preferred_element_type=jnp.float32)
        * scaling
    ).astype(jnp.bfloat16)
    keys = jnp.einsum(
        "rwc,cd->rwd", full_right, query_key, preferred_element_type=jnp.float32
    ).astype(jnp.bfloat16)
    values = jnp.einsum(
        "rwc,cd->rwd", full_right, value_weight, preferred_element_type=jnp.float32
    ).astype(jnp.bfloat16)
    block_shape = (band_count, 1, row_length, HEADS, HEAD)
    blended, shift_sums = lax.map(
        attend,
        (queries.reshape(block_shape), keys.reshape(block_shape), values.reshape(block_shape)),
    )
    head_out = blended.reshape(band_count, row_length, C)
    band_disparity = shift_sums.reshape(band_count, row_length) * (8.0 / (HEADS * row_length))
    band_occlusion = occlusion_logit(head_out, out_weight, occlusion_weight)
    maps = lax.all_to_all(
        jnp.stack([band_disparity, band_occlusion]),
        ("col", "sub"),
        split_axis=2,
        concat_axis=1,
        tiled=True,
    )
    disparity = maps[0]
    occlusion = maps[1]
    stacked = jnp.concatenate([disparity[None], occlusion[None], left_image], axis=0).astype(
        jnp.bfloat16
    )
    layer_one = jax.nn.relu(layer_same(stacked, first_conv)).astype(jnp.bfloat16)
    layer_two = jax.nn.relu(layer_same(layer_one, middle_conv[0])).astype(jnp.bfloat16)
    layer_three = jax.nn.relu(
        layer_one.astype(jnp.float32) + layer_same(layer_two, middle_conv[1])
    ).astype(jnp.bfloat16)
    layer_four = jax.nn.relu(layer_same(layer_three, middle_conv[2])).astype(jnp.bfloat16)
    correction = layer_same(layer_four, last_conv)
    disparity_out = disparity + correction[0]
    occlusion_out = jax.nn.sigmoid(occlusion + correction[1])
    return (disparity_out, occlusion_out)


def solution(mesh):
    placed = (
        P(("grp", "row"), ("col", "sub"), None),
        P(("grp", "row"), ("col", "sub"), None),
        P(None, ("grp", "row"), ("col", "sub")),
        P(),
        P(),
        P(),
        P(),
        P(),
        P(),
        P(),
    )
    return jax.shard_map(
        per_device,
        mesh=mesh,
        in_specs=placed,
        out_specs=(P(("grp", "row"), ("col", "sub")), P(("grp", "row"), ("col", "sub"))),
        check_vma=False,
    )
```

profile of v0, /device:TPU:1, one launch (start us, length us, event | category | flops | bytes accessed | tf_op | source)
XLA Modules:
  0.0 168.5 jit_solution(7081243207091826723)
XLA Ops:
  0.6 4.3 %all-to-all-start = ((bf16[32,64,128]{2,1,0:T(8,128)(2,1)}), bf16[32,64,128]{2,1,0:T(8,128)(2,1)S(1)}, u32[]{:S(2)}, u32[]{:S(2)}) async-start(bf16[32,64,128]{2,1,0:T(8,128)(2,1)} %param.13), calls=%async_computation | async-start | bytes 1048576 | tf_op jit(solution)/shard_map/all_to_all | solution.py:94
  4.9 7.8 %all-to-all-done = bf16[32,64,128]{2,1,0:T(8,128)(2,1)S(1)} async-done(((bf16[32,64,128]{2,1,0:T(8,128)(2,1)}), bf16[32,64,128]{2,1,0:T(8,128)(2,1)S(1)}, u32[]{:S(2)}, u32[]{:S(2)}) %all-to-all-start) | async-done | bytes 524320 | tf_op jit(solution)/shard_map/all_to_all | solution.py:94
  12.7 4.5 %all-to-all-start.1 = ((bf16[32,64,128]{2,1,0:T(8,128)(2,1)}), bf16[32,64,128]{2,1,0:T(8,128)(2,1)S(1)}, u32[]{:S(2)}, u32[]{:S(2)}) async-start(bf16[32,64,128]{2,1,0:T(8,128)(2,1)} %param.12), calls=%async_computation.1 | async-start | bytes 1048576 | tf_op jit(solution)/shard_map/all_to_all | solution.py:93
  19.1 6.1 %all-to-all-done.1 = bf16[32,64,128]{2,1,0:T(8,128)(2,1)S(1)} async-done(((bf16[32,64,128]{2,1,0:T(8,128)(2,1)}), bf16[32,64,128]{2,1,0:T(8,128)(2,1)S(1)}, u32[]{:S(2)}, u32[]{:S(2)}) %all-to-all-start.1) | async-done | bytes 524320 | tf_op jit(solution)/shard_map/all_to_all | solution.py:93
  25.6 36.1 %while.14 = (s32[]{:T(128)}, bf16[8,1,256,8,16]{2,4,3,1,0:T(8,128)(2,1)}, f32[8,1,256]{2,0,1:T(8,128)S(1)}, bf16[8,1,256,8,16]{2,4,3,1,0:T(8,128)(2,1)}, bf16[8,...) while((s32[]{:T(128)}, ...), condition=%wide.region_4.5_spmd.clone.clone, body=%wide.region_0.4_spmd.clone.clone.sunk | while | flops 45713408 | bytes 9060441 | solution.py:107
  28.1 2.0 %fusion.295 = bf16[8,1,256,8,16]{2,4,3,1,0:T(8,128)(2,1)} fusion(bf16[8,1,256,8,16]{2,4,3,1,0:T(8,128)(2,1)} %get-tuple-element.239, s32[]{:T(128)} %get-tuple-element.238, f32[8,256,256]{1,2,0:T(8,128)S(1)} %get-tuple-element.228, f32[8,256]{1,0:T(8,128)S(1)} %fusion.294, f32[8,256]{1,0:T(8,128)S(1)} %get-tuple-element.229, ...), kind=kOutput, calls=%fused_computation.9.clone.1 | convolution fusion | flops 18907136 | bytes 2311168 | tf_op jit(solution)/shard_map/while/body/eval_jaxpr/bhij,bjhd->bihd/dot_general | solution.py:84
  32.6 2.0 %fusion.295 = bf16[8,1,256,8,16]{2,4,3,1,0:T(8,128)(2,1)} fusion(bf16[8,1,256,8,16]{2,4,3,1,0:T(8,128)(2,1)} %get-tuple-element.239, s32[]{:T(128)} %get-tuple-element.238, f32[8,256,256]{1,2,0:T(8,128)S(1)} %get-tuple-element.228, f32[8,256]{1,0:T(8,128)S(1)} %fusion.294, f32[8,256]{1,0:T(8,128)S(1)} %get-tuple-element.229, ...), kind=kOutput, calls=%fused_computation.9.clone.1 | convolution fusion | flops 18907136 | bytes 2311168 | tf_op jit(solution)/shard_map/while/body/eval_jaxpr/bhij,bjhd->bihd/dot_general | solution.py:84
  37.1 2.0 %fusion.295 = bf16[8,1,256,8,16]{2,4,3,1,0:T(8,128)(2,1)} fusion(bf16[8,1,256,8,16]{2,4,3,1,0:T(8,128)(2,1)} %get-tuple-element.239, s32[]{:T(128)} %get-tuple-element.238, f32[8,256,256]{1,2,0:T(8,128)S(1)} %get-tuple-element.228, f32[8,256]{1,0:T(8,128)S(1)} %fusion.294, f32[8,256]{1,0:T(8,128)S(1)} %get-tuple-element.229, ...), kind=kOutput, calls=%fused_computation.9.clone.1 | convolution fusion | flops 18907136 | bytes 2311168 | tf_op jit(solution)/shard_map/while/body/eval_jaxpr/bhij,bjhd->bihd/dot_general | solution.py:84
  41.6 2.0 %fusion.295 = bf16[8,1,256,8,16]{2,4,3,1,0:T(8,128)(2,1)} fusion(bf16[8,1,256,8,16]{2,4,3,1,0:T(8,128)(2,1)} %get-tuple-element.239, s32[]{:T(128)} %get-tuple-element.238, f32[8,256,256]{1,2,0:T(8,128)S(1)} %get-tuple-element.228, f32[8,256]{1,0:T(8,128)S(1)} %fusion.294, f32[8,256]{1,0:T(8,128)S(1)} %get-tuple-element.229, ...), kind=kOutput, calls=%fused_computation.9.clone.1 | convolution fusion | flops 18907136 | bytes 2311168 | tf_op jit(solution)/shard_map/while/body/eval_jaxpr/bhij,bjhd->bihd/dot_general | solution.py:84
  46.1 2.0 %fusion.295 = bf16[8,1,256,8,16]{2,4,3,1,0:T(8,128)(2,1)} fusion(bf16[8,1,256,8,16]{2,4,3,1,0:T(8,128)(2,1)} %get-tuple-element.239, s32[]{:T(128)} %get-tuple-element.238, f32[8,256,256]{1,2,0:T(8,128)S(1)} %get-tuple-element.228, f32[8,256]{1,0:T(8,128)S(1)} %fusion.294, f32[8,256]{1,0:T(8,128)S(1)} %get-tuple-element.229, ...), kind=kOutput, calls=%fused_computation.9.clone.1 | convolution fusion | flops 18907136 | bytes 2311168 | tf_op jit(solution)/shard_map/while/body/eval_jaxpr/bhij,bjhd->bihd/dot_general | solution.py:84
  50.6 2.0 %fusion.295 = bf16[8,1,256,8,16]{2,4,3,1,0:T(8,128)(2,1)} fusion(bf16[8,1,256,8,16]{2,4,3,1,0:T(8,128)(2,1)} %get-tuple-element.239, s32[]{:T(128)} %get-tuple-element.238, f32[8,256,256]{1,2,0:T(8,128)S(1)} %get-tuple-element.228, f32[8,256]{1,0:T(8,128)S(1)} %fusion.294, f32[8,256]{1,0:T(8,128)S(1)} %get-tuple-element.229, ...), kind=kOutput, calls=%fused_computation.9.clone.1 | convolution fusion | flops 18907136 | bytes 2311168 | tf_op jit(solution)/shard_map/while/body/eval_jaxpr/bhij,bjhd->bihd/dot_general | solution.py:84
  59.6 2.0 %fusion.295 = bf16[8,1,256,8,16]{2,4,3,1,0:T(8,128)(2,1)} fusion(bf16[8,1,256,8,16]{2,4,3,1,0:T(8,128)(2,1)} %get-tuple-element.239, s32[]{:T(128)} %get-tuple-element.238, f32[8,256,256]{1,2,0:T(8,128)S(1)} %get-tuple-element.228, f32[8,256]{1,0:T(8,128)S(1)} %fusion.294, f32[8,256]{1,0:T(8,128)S(1)} %get-tuple-element.229, ...), kind=kOutput, calls=%fused_computation.9.clone.1 | convolution fusion | flops 18907136 | bytes 2311168 | tf_op jit(solution)/shard_map/while/body/eval_jaxpr/bhij,bjhd->bihd/dot_general | solution.py:84
  65.2 4.1 %all-to-all-start.2 = ((f32[4,1,1024]{2,1,0:T(1,128)}), f32[4,1,1024]{2,1,0:T(1,128)S(1)}, u32[]{:S(2)}, u32[]{:S(2)}) async-start(f32[4,1,1024]{2,1,0:T(1,128)} %reshape.211), calls=%async_computation.2 | async-start | bytes 32768 | tf_op jit(solution)/shard_map/all_to_all | solution.py:114
  69.3 3.1 %all-to-all-done.2 = f32[4,1,1024]{2,1,0:T(1,128)S(1)} async-done(((f32[4,1,1024]{2,1,0:T(1,128)}), f32[4,1,1024]{2,1,0:T(1,128)S(1)}, u32[]{:S(2)}, u32[]{:S(2)}) %all-to-all-start.2) | async-done | bytes 16416 | tf_op jit(solution)/shard_map/all_to_all | solution.py:114
  74.2 3.9 %collective-permute-start = (bf16[5,1,64]{2,1,0:T(2,128)(2,1)S(1)}, bf16[5,1,64]{2,1,0:T(2,128)(2,1)S(1)}, u32[]{:S(2)}, u32[]{:S(2)}) collective-permute-start(bf16[5,1,64]{2,1,0:T(2,128)(2,1)S(1)} %get-tuple-element.177), channel_id=1, source_target_pairs={{0,4},{4,8},{8,12},{1,5},{5,9},{9,13},{2,6},{6,10},{10,14},{3,7},{... | collective-permute-start | bytes 1928 | tf_op jit(solution)/shard_map/ppermute | solution.py:19
  79.4 3.0 %collective-permute-done.1 = bf16[5,1,64]{2,1,0:T(2,128)(2,1)S(1)} collective-permute-done((bf16[5,1,64]{2,1,0:T(2,128)(2,1)S(1)}, bf16[5,1,64]{2,1,0:T(2,128)(2,1)S(1)}, u32[]{:S(2)}, u32[]{:S(2)}) %collective-permute-start.1) | collective-permute-done | bytes 672 | tf_op jit(solution)/shard_map/ppermute | solution.py:21
  82.6 3.7 %collective-permute-start.2 = (bf16[5,34,1]{2,1,0:T(8,128)(2,1)S(1)}, bf16[5,34,1]{2,1,0:T(8,128)(2,1)S(1)}, u32[]{:S(2)}, u32[]{:S(2)}) collective-permute-start(bf16[5,34,1]{2,1,0:T(8,128)(2,1)S(1)} %get-tuple-element.171), channel_id=1, source_target_pairs={{0,1},{1,2},{2,3},{4,5},{5,6},{6,7},{8,9},{9,10},{10,11},{12,13},{... | collective-permute-start | bytes 1028 | tf_op jit(solution)/shard_map/ppermute | solution.py:19
  88.6 3.1 %collective-permute-done.3 = bf16[5,34,1]{2,1,0:T(8,128)(2,1)S(1)} collective-permute-done((bf16[5,34,1]{2,1,0:T(8,128)(2,1)S(1)}, bf16[5,34,1]{2,1,0:T(8,128)(2,1)S(1)}, u32[]{:S(2)}, u32[]{:S(2)}) %collective-permute-start.3) | collective-permute-done | bytes 372 | tf_op jit(solution)/shard_map/ppermute | solution.py:21
  94.8 3.2 %collective-permute-start.4 = (bf16[64,1,64]{0,2,1:T(8,128)(2,1)S(1)}, bf16[64,1,64]{0,2,1:T(8,128)(2,1)S(1)}, u32[]{:S(2)}, u32[]{:S(2)}) collective-permute-start(bf16[64,1,64]{0,2,1:T(8,128)(2,1)S(1)} %get-tuple-element.163), channel_id=1, source_target_pairs={{0,4},{4,8},{8,12},{1,5},{5,9},{9,13},{2,6},{6,10},{10,14},{3,7},{... | collective-permute-start | bytes 24584 | tf_op jit(solution)/shard_map/ppermute | solution.py:19
  99.7 2.9 %collective-permute-done.5 = bf16[64,1,64]{0,2,1:T(8,128)(2,1)S(1)} collective-permute-done((bf16[64,1,64]{0,2,1:T(8,128)(2,1)S(1)}, bf16[64,1,64]{0,2,1:T(8,128)(2,1)S(1)}, u32[]{:S(2)}, u32[]{:S(2)}) %collective-permute-start.5) | collective-permute-done | bytes 8224 | tf_op jit(solution)/shard_map/ppermute | solution.py:21
  102.6 3.3 %collective-permute-start.6 = (bf16[64,34,1]{0,2,1:T(2,128)(2,1)S(1)}, bf16[64,34,1]{0,2,1:T(2,128)(2,1)S(1)}, u32[]{:S(2)}, u32[]{:S(2)}) collective-permute-start(bf16[64,34,1]{0,2,1:T(2,128)(2,1)S(1)} %get-tuple-element.155), channel_id=1, source_target_pairs={{0,1},{1,2},{2,3},{4,5},{5,6},{6,7},{8,9},{9,10},{10,11},{12,13},{... | collective-permute-start | bytes 13064 | tf_op jit(solution)/shard_map/ppermute | solution.py:19
  108.4 2.5 %collective-permute-done.7 = bf16[64,34,1]{0,2,1:T(2,128)(2,1)S(1)} collective-permute-done((bf16[64,34,1]{0,2,1:T(2,128)(2,1)S(1)}, bf16[64,34,1]{0,2,1:T(2,128)(2,1)S(1)}, u32[]{:S(2)}, u32[]{:S(2)}) %collective-permute-start.7) | collective-permute-done | bytes 4384 | tf_op jit(solution)/shard_map/ppermute | solution.py:21
  113.3 3.4 %collective-permute-start.8 = (bf16[64,1,64]{0,2,1:T(8,128)(2,1)S(1)}, bf16[64,1,64]{0,2,1:T(8,128)(2,1)S(1)}, u32[]{:S(2)}, u32[]{:S(2)}) collective-permute-start(bf16[64,1,64]{0,2,1:T(8,128)(2,1)S(1)} %get-tuple-element.161), channel_id=1, source_target_pairs={{0,4},{4,8},{8,12},{1,5},{5,9},{9,13},{2,6},{6,10},{10,14},{3,7},{... | collective-permute-start | bytes 24584 | tf_op jit(solution)/shard_map/ppermute | solution.py:19
  118.3 2.9 %collective-permute-done.9 = bf16[64,1,64]{0,2,1:T(8,128)(2,1)S(1)} collective-permute-done((bf16[64,1,64]{0,2,1:T(8,128)(2,1)S(1)}, bf16[64,1,64]{0,2,1:T(8,128)(2,1)S(1)}, u32[]{:S(2)}, u32[]{:S(2)}) %collective-permute-start.9) | collective-permute-done | bytes 8224 | tf_op jit(solution)/shard_map/ppermute | solution.py:21
  121.3 3.4 %collective-permute-start.10 = (bf16[64,34,1]{0,2,1:T(2,128)(2,1)S(1)}, bf16[64,34,1]{0,2,1:T(2,128)(2,1)S(1)}, u32[]{:S(2)}, u32[]{:S(2)}) collective-permute-start(bf16[64,34,1]{0,2,1:T(2,128)(2,1)S(1)} %get-tuple-element.151), channel_id=1, source_target_pairs={{0,1},{1,2},{2,3},{4,5},{5,6},{6,7},{8,9},{9,10},{10,11},{12,13},{... | collective-permute-start | bytes 13064 | tf_op jit(solution)/shard_map/ppermute | solution.py:19
  127.2 2.5 %collective-permute-done.11 = bf16[64,34,1]{0,2,1:T(2,128)(2,1)S(1)} collective-permute-done((bf16[64,34,1]{0,2,1:T(2,128)(2,1)S(1)}, bf16[64,34,1]{0,2,1:T(2,128)(2,1)S(1)}, u32[]{:S(2)}, u32[]{:S(2)}) %collective-permute-start.11) | collective-permute-done | bytes 4384 | tf_op jit(solution)/shard_map/ppermute | solution.py:21
  135.4 2.9 %collective-permute-done.13 = bf16[64,1,64]{0,2,1:T(8,128)(2,1)S(1)} collective-permute-done((bf16[64,1,64]{0,2,1:T(8,128)(2,1)S(1)}, bf16[64,1,64]{0,2,1:T(8,128)(2,1)S(1)}, u32[]{:S(2)}, u32[]{:S(2)}) %collective-permute-start.13) | collective-permute-done | bytes 8224 | tf_op jit(solution)/shard_map/ppermute | solution.py:21
  138.4 3.4 %collective-permute-start.14 = (bf16[64,34,1]{0,2,1:T(2,128)(2,1)S(1)}, bf16[64,34,1]{0,2,1:T(2,128)(2,1)S(1)}, u32[]{:S(2)}, u32[]{:S(2)}) collective-permute-start(bf16[64,34,1]{0,2,1:T(2,128)(2,1)S(1)} %get-tuple-element.147), channel_id=1, source_target_pairs={{0,1},{1,2},{2,3},{4,5},{5,6},{6,7},{8,9},{9,10},{10,11},{12,13},{... | collective-permute-start | bytes 13064 | tf_op jit(solution)/shard_map/ppermute | solution.py:19
  144.3 2.5 %collective-permute-done.15 = bf16[64,34,1]{0,2,1:T(2,128)(2,1)S(1)} collective-permute-done((bf16[64,34,1]{0,2,1:T(2,128)(2,1)S(1)}, bf16[64,34,1]{0,2,1:T(2,128)(2,1)S(1)}, u32[]{:S(2)}, u32[]{:S(2)}) %collective-permute-start.15) | collective-permute-done | bytes 4384 | tf_op jit(solution)/shard_map/ppermute | solution.py:21
  152.6 2.7 %collective-permute-done.17 = bf16[64,1,64]{0,2,1:T(8,128)(2,1)S(1)} collective-permute-done((bf16[64,1,64]{0,2,1:T(8,128)(2,1)S(1)}, bf16[64,1,64]{0,2,1:T(8,128)(2,1)S(1)}, u32[]{:S(2)}, u32[]{:S(2)}) %collective-permute-start.17) | collective-permute-done | bytes 8224 | tf_op jit(solution)/shard_map/ppermute | solution.py:21
  155.4 3.4 %collective-permute-start.18 = (bf16[64,34,1]{0,2,1:T(2,128)(2,1)S(1)}, bf16[64,34,1]{0,2,1:T(2,128)(2,1)S(1)}, u32[]{:S(2)}, u32[]{:S(2)}) collective-permute-start(bf16[64,34,1]{0,2,1:T(2,128)(2,1)S(1)} %get-tuple-element.143), channel_id=1, source_target_pairs={{0,1},{1,2},{2,3},{4,5},{5,6},{6,7},{8,9},{9,10},{10,11},{12,13},{... | collective-permute-start | bytes 13064 | tf_op jit(solution)/shard_map/ppermute | solution.py:19
  161.7 2.1 %collective-permute-done.19 = bf16[64,34,1]{0,2,1:T(2,128)(2,1)S(1)} collective-permute-done((bf16[64,34,1]{0,2,1:T(2,128)(2,1)S(1)}, bf16[64,34,1]{0,2,1:T(2,128)(2,1)S(1)}, u32[]{:S(2)}, u32[]{:S(2)}) %collective-permute-start.19) | collective-permute-done | bytes 4384 | tf_op jit(solution)/shard_map/ppermute | solution.py:21
  (188 shorter events, 68.1 us)
Async XLA Ops:
  0.6 16.6 %copy-start = (bf16[128,128]{1,0:T(8,128)(2,1)S(1)}, bf16[128,128]{1,0:T(8,128)(2,1)}, u32[]{:S(2)}) copy-start(bf16[128,128]{1,0:T(8,128)(2,1)} %param.15) | copy-start | bytes 98308
  0.6 12.1 %all-to-all-start = ((bf16[32,64,128]{2,1,0:T(8,128)(2,1)}), bf16[32,64,128]{2,1,0:T(8,128)(2,1)S(1)}, u32[]{:S(2)}, u32[]{:S(2)}) async-start(bf16[32,64,128]{2,1,0:T(8,128)(2,1)} %param.13), calls=%async_computation | async-start | bytes 1048576 | tf_op jit(solution)/shard_map/all_to_all | solution.py:94
  12.7 12.5 %all-to-all-start.1 = ((bf16[32,64,128]{2,1,0:T(8,128)(2,1)}), bf16[32,64,128]{2,1,0:T(8,128)(2,1)S(1)}, u32[]{:S(2)}, u32[]{:S(2)}) async-start(bf16[32,64,128]{2,1,0:T(8,128)(2,1)} %param.12), calls=%async_computation.1 | async-start | bytes 1048576 | tf_op jit(solution)/shard_map/all_to_all | solution.py:93
  17.2 0.8 copy-start.3
  25.6 36.1 %copy-start.4 = (bf16[128,128]{1,0:T(8,128)(2,1)S(1)}, bf16[128,128]{1,0:T(8,128)(2,1)}, u32[]{:S(2)}) copy-start(bf16[128,128]{1,0:T(8,128)(2,1)} %param.17) | copy-start | bytes 98308
  61.7 1.6 copy-start.6
  63.1 6.2 %copy-start.2 = (f32[3,32,64]{2,1,0:T(8,128)S(1)}, f32[3,32,64]{2,1,0:T(8,128)}, u32[]{:S(2)}) copy-start(f32[3,32,64]{2,1,0:T(8,128)} %param.14) | copy-start | bytes 73732
  64.0 24.3 %copy-start.5 = (bf16[9,64,5]{1,2,0:T(8,128)(2,1)S(1)}, bf16[9,64,5]{1,2,0:T(8,128)(2,1)}, u32[]{:S(2)}) copy-start(bf16[9,64,5]{1,2,0:T(8,128)(2,1)} %param.19) | copy-start | bytes 17284
  65.2 7.2 %all-to-all-start.2 = ((f32[4,1,1024]{2,1,0:T(1,128)}), f32[4,1,1024]{2,1,0:T(1,128)S(1)}, u32[]{:S(2)}, u32[]{:S(2)}) async-start(f32[4,1,1024]{2,1,0:T(1,128)} %reshape.211), calls=%async_computation.2 | async-start | bytes 32768 | tf_op jit(solution)/shard_map/all_to_all | solution.py:114
  74.2 5.2 %collective-permute-start = (bf16[5,1,64]{2,1,0:T(2,128)(2,1)S(1)}, bf16[5,1,64]{2,1,0:T(2,128)(2,1)S(1)}, u32[]{:S(2)}, u32[]{:S(2)}) collective-permute-start(bf16[5,1,64]{2,1,0:T(2,128)(2,1)S(1)} %get-tuple-element.177), channel_id=1, source_target_pairs={{0,4},{4,8},{8,12},{1,5},{5,9},{9,13},{2,6},{6,10},{10,14},{3,7},{... | collective-permute-start | bytes 1928 | tf_op jit(solution)/shard_map/ppermute | solution.py:19
  78.1 4.3 %collective-permute-start.1 = (bf16[5,1,64]{2,1,0:T(2,128)(2,1)S(1)}, bf16[5,1,64]{2,1,0:T(2,128)(2,1)S(1)}, u32[]{:S(2)}, u32[]{:S(2)}) collective-permute-start(bf16[5,1,64]{2,1,0:T(2,128)(2,1)S(1)} %get-tuple-element.178), channel_id=1, source_target_pairs={{4,0},{8,4},{12,8},{5,1},{9,5},{13,9},{6,2},{10,6},{14,10},{7,3},{... | collective-permute-start | bytes 1928 | tf_op jit(solution)/shard_map/ppermute | solution.py:21
  82.6 6.0 %collective-permute-start.2 = (bf16[5,34,1]{2,1,0:T(8,128)(2,1)S(1)}, bf16[5,34,1]{2,1,0:T(8,128)(2,1)S(1)}, u32[]{:S(2)}, u32[]{:S(2)}) collective-permute-start(bf16[5,34,1]{2,1,0:T(8,128)(2,1)S(1)} %get-tuple-element.171), channel_id=1, source_target_pairs={{0,1},{1,2},{2,3},{4,5},{5,6},{6,7},{8,9},{9,10},{10,11},{12,13},{... | collective-permute-start | bytes 1028 | tf_op jit(solution)/shard_map/ppermute | solution.py:19
  86.3 5.4 %collective-permute-start.3 = (bf16[5,34,1]{2,1,0:T(8,128)(2,1)S(1)}, bf16[5,34,1]{2,1,0:T(8,128)(2,1)S(1)}, u32[]{:S(2)}, u32[]{:S(2)}) collective-permute-start(bf16[5,34,1]{2,1,0:T(8,128)(2,1)S(1)} %get-tuple-element.172), channel_id=1, source_target_pairs={{1,0},{2,1},{3,2},{5,4},{6,5},{7,6},{9,8},{10,9},{11,10},{13,12},{... | collective-permute-start | bytes 1028 | tf_op jit(solution)/shard_map/ppermute | solution.py:21
  94.4 4.9 %copy-start.1 = (bf16[3,9,64,64]{3,2,1,0:T(8,128)(2,1)S(1)}, bf16[3,9,64,64]{3,2,1,0:T(8,128)(2,1)}, u32[]{:S(2)}) copy-start(bf16[3,9,64,64]{3,2,1,0:T(8,128)(2,1)} %param.20) | copy-start | bytes 663556
  94.8 4.8 %collective-permute-start.4 = (bf16[64,1,64]{0,2,1:T(8,128)(2,1)S(1)}, bf16[64,1,64]{0,2,1:T(8,128)(2,1)S(1)}, u32[]{:S(2)}, u32[]{:S(2)}) collective-permute-start(bf16[64,1,64]{0,2,1:T(8,128)(2,1)S(1)} %get-tuple-element.163), channel_id=1, source_target_pairs={{0,4},{4,8},{8,12},{1,5},{5,9},{9,13},{2,6},{6,10},{10,14},{3,7},{... | collective-permute-start | bytes 24584 | tf_op jit(solution)/shard_map/ppermute | solution.py:19
  98.0 4.5 %collective-permute-start.5 = (bf16[64,1,64]{0,2,1:T(8,128)(2,1)S(1)}, bf16[64,1,64]{0,2,1:T(8,128)(2,1)S(1)}, u32[]{:S(2)}, u32[]{:S(2)}) collective-permute-start(bf16[64,1,64]{0,2,1:T(8,128)(2,1)S(1)} %get-tuple-element.164), channel_id=1, source_target_pairs={{4,0},{8,4},{12,8},{5,1},{9,5},{13,9},{6,2},{10,6},{14,10},{7,3},{... | collective-permute-start | bytes 24584 | tf_op jit(solution)/shard_map/ppermute | solution.py:21
  102.6 5.9 %collective-permute-start.6 = (bf16[64,34,1]{0,2,1:T(2,128)(2,1)S(1)}, bf16[64,34,1]{0,2,1:T(2,128)(2,1)S(1)}, u32[]{:S(2)}, u32[]{:S(2)}) collective-permute-start(bf16[64,34,1]{0,2,1:T(2,128)(2,1)S(1)} %get-tuple-element.155), channel_id=1, source_target_pairs={{0,1},{1,2},{2,3},{4,5},{5,6},{6,7},{8,9},{9,10},{10,11},{12,13},{... | collective-permute-start | bytes 13064 | tf_op jit(solution)/shard_map/ppermute | solution.py:19
  105.9 5.1 %collective-permute-start.7 = (bf16[64,34,1]{0,2,1:T(2,128)(2,1)S(1)}, bf16[64,34,1]{0,2,1:T(2,128)(2,1)S(1)}, u32[]{:S(2)}, u32[]{:S(2)}) collective-permute-start(bf16[64,34,1]{0,2,1:T(2,128)(2,1)S(1)} %get-tuple-element.156), channel_id=1, source_target_pairs={{1,0},{2,1},{3,2},{5,4},{6,5},{7,6},{9,8},{10,9},{11,10},{13,12},{... | collective-permute-start | bytes 13064 | tf_op jit(solution)/shard_map/ppermute | solution.py:21
  113.3 5.0 %collective-permute-start.8 = (bf16[64,1,64]{0,2,1:T(8,128)(2,1)S(1)}, bf16[64,1,64]{0,2,1:T(8,128)(2,1)S(1)}, u32[]{:S(2)}, u32[]{:S(2)}) collective-permute-start(bf16[64,1,64]{0,2,1:T(8,128)(2,1)S(1)} %get-tuple-element.161), channel_id=1, source_target_pairs={{0,4},{4,8},{8,12},{1,5},{5,9},{9,13},{2,6},{6,10},{10,14},{3,7},{... | collective-permute-start | bytes 24584 | tf_op jit(solution)/shard_map/ppermute | solution.py:19
  116.7 4.5 %collective-permute-start.9 = (bf16[64,1,64]{0,2,1:T(8,128)(2,1)S(1)}, bf16[64,1,64]{0,2,1:T(8,128)(2,1)S(1)}, u32[]{:S(2)}, u32[]{:S(2)}) collective-permute-start(bf16[64,1,64]{0,2,1:T(8,128)(2,1)S(1)} %get-tuple-element.162), channel_id=1, source_target_pairs={{4,0},{8,4},{12,8},{5,1},{9,5},{13,9},{6,2},{10,6},{14,10},{7,3},{... | collective-permute-start | bytes 24584 | tf_op jit(solution)/shard_map/ppermute | solution.py:21
  121.3 5.9 %collective-permute-start.10 = (bf16[64,34,1]{0,2,1:T(2,128)(2,1)S(1)}, bf16[64,34,1]{0,2,1:T(2,128)(2,1)S(1)}, u32[]{:S(2)}, u32[]{:S(2)}) collective-permute-start(bf16[64,34,1]{0,2,1:T(2,128)(2,1)S(1)} %get-tuple-element.151), channel_id=1, source_target_pairs={{0,1},{1,2},{2,3},{4,5},{5,6},{6,7},{8,9},{9,10},{10,11},{12,13},{... | collective-permute-start | bytes 13064 | tf_op jit(solution)/shard_map/ppermute | solution.py:19
  124.6 5.1 %collective-permute-start.11 = (bf16[64,34,1]{0,2,1:T(2,128)(2,1)S(1)}, bf16[64,34,1]{0,2,1:T(2,128)(2,1)S(1)}, u32[]{:S(2)}, u32[]{:S(2)}) collective-permute-start(bf16[64,34,1]{0,2,1:T(2,128)(2,1)S(1)} %get-tuple-element.152), channel_id=1, source_target_pairs={{1,0},{2,1},{3,2},{5,4},{6,5},{7,6},{9,8},{10,9},{11,10},{13,12},{... | collective-permute-start | bytes 13064 | tf_op jit(solution)/shard_map/ppermute | solution.py:21
  132.2 3.2 %collective-permute-start.12 = (bf16[64,1,64]{0,2,1:T(8,128)(2,1)S(1)}, bf16[64,1,64]{0,2,1:T(8,128)(2,1)S(1)}, u32[]{:S(2)}, u32[]{:S(2)}) collective-permute-start(bf16[64,1,64]{0,2,1:T(8,128)(2,1)S(1)} %get-tuple-element.159), channel_id=1, source_target_pairs={{0,4},{4,8},{8,12},{1,5},{5,9},{9,13},{2,6},{6,10},{10,14},{3,7},{... | collective-permute-start | bytes 24584 | tf_op jit(solution)/shard_map/ppermute | solution.py:19
  133.8 4.5 %collective-permute-start.13 = (bf16[64,1,64]{0,2,1:T(8,128)(2,1)S(1)}, bf16[64,1,64]{0,2,1:T(8,128)(2,1)S(1)}, u32[]{:S(2)}, u32[]{:S(2)}) collective-permute-start(bf16[64,1,64]{0,2,1:T(8,128)(2,1)S(1)} %get-tuple-element.160), channel_id=1, source_target_pairs={{4,0},{8,4},{12,8},{5,1},{9,5},{13,9},{6,2},{10,6},{14,10},{7,3},{... | collective-permute-start | bytes 24584 | tf_op jit(solution)/shard_map/ppermute | solution.py:21
  138.4 5.9 %collective-permute-start.14 = (bf16[64,34,1]{0,2,1:T(2,128)(2,1)S(1)}, bf16[64,34,1]{0,2,1:T(2,128)(2,1)S(1)}, u32[]{:S(2)}, u32[]{:S(2)}) collective-permute-start(bf16[64,34,1]{0,2,1:T(2,128)(2,1)S(1)} %get-tuple-element.147), channel_id=1, source_target_pairs={{0,1},{1,2},{2,3},{4,5},{5,6},{6,7},{8,9},{9,10},{10,11},{12,13},{... | collective-permute-start | bytes 13064 | tf_op jit(solution)/shard_map/ppermute | solution.py:19
  141.7 5.1 %collective-permute-start.15 = (bf16[64,34,1]{0,2,1:T(2,128)(2,1)S(1)}, bf16[64,34,1]{0,2,1:T(2,128)(2,1)S(1)}, u32[]{:S(2)}, u32[]{:S(2)}) collective-permute-start(bf16[64,34,1]{0,2,1:T(2,128)(2,1)S(1)} %get-tuple-element.148), channel_id=1, source_target_pairs={{1,0},{2,1},{3,2},{5,4},{6,5},{7,6},{9,8},{10,9},{11,10},{13,12},{... | collective-permute-start | bytes 13064 | tf_op jit(solution)/shard_map/ppermute | solution.py:21
  148.7 3.4 %copy-start.7 = (bf16[9,2,64]{2,1,0:T(2,128)(2,1)S(1)}, bf16[9,2,64]{2,1,0:T(2,128)(2,1)}, u32[]{:S(2)}) copy-start(bf16[9,2,64]{2,1,0:T(2,128)(2,1)} %param.21) | copy-start | bytes 6916
  149.2 3.5 %collective-permute-start.16 = (bf16[64,1,64]{0,2,1:T(8,128)(2,1)S(1)}, bf16[64,1,64]{0,2,1:T(8,128)(2,1)S(1)}, u32[]{:S(2)}, u32[]{:S(2)}) collective-permute-start(bf16[64,1,64]{0,2,1:T(8,128)(2,1)S(1)} %get-tuple-element.157), channel_id=1, source_target_pairs={{0,4},{4,8},{8,12},{1,5},{5,9},{9,13},{2,6},{6,10},{10,14},{3,7},{... | collective-permute-start | bytes 24584 | tf_op jit(solution)/shard_map/ppermute | solution.py:19
  150.8 4.5 %collective-permute-start.17 = (bf16[64,1,64]{0,2,1:T(8,128)(2,1)S(1)}, bf16[64,1,64]{0,2,1:T(8,128)(2,1)S(1)}, u32[]{:S(2)}, u32[]{:S(2)}) collective-permute-start(bf16[64,1,64]{0,2,1:T(8,128)(2,1)S(1)} %get-tuple-element.158), channel_id=1, source_target_pairs={{4,0},{8,4},{12,8},{5,1},{9,5},{13,9},{6,2},{10,6},{14,10},{7,3},{... | collective-permute-start | bytes 24584 | tf_op jit(solution)/shard_map/ppermute | solution.py:21
  155.4 6.3 %collective-permute-start.18 = (bf16[64,34,1]{0,2,1:T(2,128)(2,1)S(1)}, bf16[64,34,1]{0,2,1:T(2,128)(2,1)S(1)}, u32[]{:S(2)}, u32[]{:S(2)}) collective-permute-start(bf16[64,34,1]{0,2,1:T(2,128)(2,1)S(1)} %get-tuple-element.143), channel_id=1, source_target_pairs={{0,1},{1,2},{2,3},{4,5},{5,6},{6,7},{8,9},{9,10},{10,11},{12,13},{... | collective-permute-start | bytes 13064 | tf_op jit(solution)/shard_map/ppermute | solution.py:19
  158.7 5.1 %collective-permute-start.19 = (bf16[64,34,1]{0,2,1:T(2,128)(2,1)S(1)}, bf16[64,34,1]{0,2,1:T(2,128)(2,1)S(1)}, u32[]{:S(2)}, u32[]{:S(2)}) collective-permute-start(bf16[64,34,1]{0,2,1:T(2,128)(2,1)S(1)} %get-tuple-element.144), channel_id=1, source_target_pairs={{1,0},{2,1},{3,2},{5,4},{6,5},{7,6},{9,8},{10,9},{11,10},{13,12},{... | collective-permute-start | bytes 13064 | tf_op jit(solution)/shard_map/ppermute | solution.py:21
where the time goes:
time: 170 us; the launch traced here: 168 us
  starting transfers between devices  59.8 us (35%)
  matrix products  52.6 us (31%)
  waiting for transfers between devices  44.1 us (26%)
  other arithmetic  6.97 us (4%)
  local copies, waits for them, and re-layouts  3.3 us (2%)
    ppermute x10, starting transfers between devices, with_halo(): lax.ppermute(tail, axis, [(i, (i + 1) % count) for i in range(ends)])  30.9 us
    ppermute x10, waiting for transfers between devices, with_halo(): lax.ppermute(head, axis, [((i + 1) % count, i) for i in range(ends)])  27.1 us
    dot_general x45, matrix products, conv_valid(): jnp.einsum('oc,crw->orw', weight[offset], window, preferred_element_type=...  16.7 us
    dot_general x8, matrix products, attend(): jnp.einsum('bhij,bjhd->bihd', probabilities, value_block, preferred_eleme...  16.1 us
    ppermute x10, starting transfers between devices, with_halo(): lax.ppermute(head, axis, [((i + 1) % count, i) for i in range(ends)])  16.1 us
    dot_general x8, matrix products, attend(): jnp.einsum('bhij,j->bhi', exponent, places, precision=lax.Precision.HIGHEST)  11.8 us
    all_to_all x1, waiting for transfers between devices, per_device(): lax.all_to_all(right_features, ('col', 'sub'), split_axis=0, concat_axis=...  7.79 us
    all_to_all x1, waiting for transfers between devices, per_device(): lax.all_to_all(left_features, ('col', 'sub'), split_axis=0, concat_axis=1...  6.1 us
  transfers between devices with their start and end apart: 23, of which 13 were waited for; matrix products, arithmetic and copies ran while one was open for 4% of the time, Pallas kernels for 0%

commit v1 on v0

--- a/solution.py
+++ b/solution.py
@@ -6,6 +6,18 @@
 C = 128
 HEADS = 8
 HEAD = 16
+
+
+def cut_along(value, dim, count):
+    lengths = value.shape
+    blocks = value.reshape(*lengths[:dim], count, lengths[dim] // count, *lengths[dim + 1 :])
+    return jnp.moveaxis(blocks, dim, 0)
+
+
+def in_order(pieces, dim):
+    pieces = jnp.moveaxis(pieces, 0, dim)
+    shape = pieces.shape
+    return pieces.reshape(*shape[:dim], shape[dim] * shape[dim + 1], *shape[dim + 2 :])
 
 
 def with_halo(cells, sides, width):
@@ -111,13 +123,18 @@
     head_out = blended.reshape(band_count, row_length, C)
     band_disparity = shift_sums.reshape(band_count, row_length) * (8.0 / (HEADS * row_length))
     band_occlusion = occlusion_logit(head_out, out_weight, occlusion_weight)
-    maps = lax.all_to_all(
-        jnp.stack([band_disparity, band_occlusion]),
-        ("col", "sub"),
-        split_axis=2,
-        concat_axis=1,
-        tiled=True,
-    )
+    x = jnp.stack([band_disparity, band_occlusion])
+    devices, index = (lax.axis_size(("col", "sub")), lax.axis_index(("col", "sub")))
+    blocks = cut_along(x, 2, devices)
+    result = blocks
+    for step in range(1, devices):
+        target, source_2 = ((index + step) % devices, (index - step) % devices)
+        sent = lax.dynamic_index_in_dim(blocks, target, 0)
+        received = lax.ppermute(
+            sent, ("col", "sub"), [(i_2, (i_2 + step) % devices) for i_2 in range(devices)]
+        )
+        result = lax.dynamic_update_slice_in_dim(result, received, source_2, axis=0)
+    maps = in_order(result, 1)
     disparity = maps[0]
     occlusion = maps[1]
     stacked = jnp.concatenate([disparity[None], occlusion[None], left_image], axis=0).astype(

time: 170 us -> 152 us (0.89)
  matrix products: 52.6 us -> 39.1 us
  local copies, waits for them, and re-layouts: 3.3 us -> 1.36 us
  waiting for transfers between devices: 44.1 us -> 42.3 us
    dot_general x8, matrix products: 16.1 us -> 4.49 us  [attend(): jnp.einsum('bhij,bjhd->bihd', probabilities, value_block, preferred_eleme...]
    all_to_all x1 -> x0, starting transfers between devices: 4.1 us -> none  [per_device(): lax.all_to_all(jnp.stack([band_disparity, band_occlusion]), ('col', 'sub'...]
    all_to_all x1 -> x0, waiting for transfers between devices: 3.12 us -> none  [per_device(): lax.all_to_all(jnp.stack([band_disparity, band_occlusion]), ('col', 'sub'...]
    ppermute x0 -> x3, waiting for transfers between devices: none -> 2.92 us  [per_device(): lax.ppermute(sent, ('col', 'sub'), [(i_2, (i_2 + step) % devices) for i_2...]
    ppermute x10, waiting for transfers between devices: 27.1 us -> 24.4 us  [with_halo(): lax.ppermute(head, axis, [((i + 1) % count, i) for i in range(ends)])]
    ppermute x10, starting transfers between devices: 30.9 us -> 33.2 us  [with_halo(): lax.ppermute(tail, axis, [(i, (i + 1) % count) for i in range(ends)])]
    ppermute x0 -> x3, starting transfers between devices: none -> 2.28 us  [per_device(): lax.ppermute(sent, ('col', 'sub'), [(i_2, (i_2 + step) % devices) for i_2...]
  transfers between devices with their start and end apart: 23 -> 25, of which waited for: 13 -> 14; matrix products, arithmetic and copies ran while one was open for 4% -> 4% of each run, Pallas kernels for 0% -> 0%
where the time goes in v1:
time: 152 us; the launch traced here: 151 us
  starting transfers between devices  60.5 us (40%)
  waiting for transfers between devices  42.3 us (28%)
  matrix products  39.1 us (26%)
  other arithmetic  6.3 us (4%)
    ppermute x10, starting transfers between devices, with_halo(): lax.ppermute(tail, axis, [(i, (i + 1) % count) for i in range(ends)])  33.2 us
    ppermute x10, waiting for transfers between devices, with_halo(): lax.ppermute(head, axis, [((i + 1) % count, i) for i in range(ends)])  24.4 us
    dot_general x45, matrix products, conv_valid(): jnp.einsum('oc,crw->orw', weight[offset], window, preferred_element_type=...  16.7 us
    ppermute x10, starting transfers between devices, with_halo(): lax.ppermute(head, axis, [((i + 1) % count, i) for i in range(ends)])  16.2 us
    dot_general x8, matrix products, attend(): jnp.einsum('bhij,j->bhi', exponent, places, precision=lax.Precision.HIGHEST)  11.8 us
    all_to_all x1, waiting for transfers between devices, per_device(): lax.all_to_all(right_features, ('col', 'sub'), split_axis=0, concat_axis=...  7.79 us
    all_to_all x1, waiting for transfers between devices, per_device(): lax.all_to_all(left_features, ('col', 'sub'), split_axis=0, concat_axis=1...  6.88 us
    all_to_all x1, starting transfers between devices, per_device(): lax.all_to_all(left_features, ('col', 'sub'), split_axis=0, concat_axis=1...  4.49 us
  transfers between devices with their start and end apart: 25, of which 14 were waited for; matrix products, arithmetic and copies ran while one was open for 4% of the time, Pallas kernels for 0%

profile of v1, /device:TPU:1, one launch (start us, length us, event | category | flops | bytes accessed | tf_op | source)
XLA Modules:
  0.0 151.3 jit_solution(1694078275800073438)
XLA Ops:
  0.6 4.3 %all-to-all-start = ((bf16[32,64,128]{2,1,0:T(8,128)(2,1)}), bf16[32,64,128]{2,1,0:T(8,128)(2,1)S(1)}, u32[]{:S(2)}, u32[]{:S(2)}) async-start(bf16[32,64,128]{2,1,0:T(8,128)(2,1)} %param.13), calls=%async_computation | async-start | bytes 1048576 | tf_op jit(solution)/shard_map/all_to_all | solution.py:106
  4.9 7.8 %all-to-all-done = bf16[32,64,128]{2,1,0:T(8,128)(2,1)S(1)} async-done(((bf16[32,64,128]{2,1,0:T(8,128)(2,1)}), bf16[32,64,128]{2,1,0:T(8,128)(2,1)S(1)}, u32[]{:S(2)}, u32[]{:S(2)}) %all-to-all-start) | async-done | bytes 524320 | tf_op jit(solution)/shard_map/all_to_all | solution.py:106
  12.7 4.5 %all-to-all-start.1 = ((bf16[32,64,128]{2,1,0:T(8,128)(2,1)}), bf16[32,64,128]{2,1,0:T(8,128)(2,1)S(1)}, u32[]{:S(2)}, u32[]{:S(2)}) async-start(bf16[32,64,128]{2,1,0:T(8,128)(2,1)} %param.12), calls=%async_computation.1 | async-start | bytes 1048576 | tf_op jit(solution)/shard_map/all_to_all | solution.py:105
  18.3 6.9 %all-to-all-done.1 = bf16[32,64,128]{2,1,0:T(8,128)(2,1)S(1)} async-done(((bf16[32,64,128]{2,1,0:T(8,128)(2,1)}), bf16[32,64,128]{2,1,0:T(8,128)(2,1)S(1)}, u32[]{:S(2)}, u32[]{:S(2)}) %all-to-all-start.1) | async-done | bytes 524320 | tf_op jit(solution)/shard_map/all_to_all | solution.py:105
  25.6 24.2 %while.14 = (s32[]{:T(128)}, bf16[8,1,256,8,16]{2,4,3,1,0:T(8,128)(2,1)S(1)}, f32[8,1,256]{2,1,0:T(1,128)S(1)}, bf16[8,1,256,8,16]{2,4,3,1,0:T(8,128)(2,1)S(1)},...) while((s32[]{:T(128)}, ...), condition=%wide.region_4.5_spmd.clone.clone, body=%wide.region_0.4_spmd.clone.clone.sunk | while | flops 45713408 | bytes 9060433 | solution.py:119
  29.2 1.5 fusion.296
  32.2 1.5 fusion.296
  55.1 1.7 %collective-permute-done.2 = f32[1,2,8,64]{3,0,2,1:T(1,128)S(1)} collective-permute-done((f32[1,2,8,64]{3,0,2,1:T(1,128)S(1)}, f32[1,2,8,64]{3,0,2,1:T(1,128)S(1)}, u32[]{:S(2)}, u32[]{:S(2)}) %collective-permute-start.2) | collective-permute-done | bytes 4128 | tf_op jit(solution)/shard_map/ppermute | solution.py:133
  56.9 3.9 %collective-permute-start.3 = (bf16[5,1,64]{2,1,0:T(2,128)(2,1)S(1)}, bf16[5,1,64]{2,1,0:T(2,128)(2,1)S(1)}, u32[]{:S(2)}, u32[]{:S(2)}) collective-permute-start(bf16[5,1,64]{2,1,0:T(2,128)(2,1)S(1)} %get-tuple-element.153), channel_id=1, source_target_pairs={{0,4},{4,8},{8,12},{1,5},{5,9},{9,13},{2,6},{6,10},{10,14},{3,7},{... | collective-permute-start | bytes 1928 | tf_op jit(solution)/shard_map/ppermute | solution.py:31
  62.1 3.0 %collective-permute-done.4 = bf16[5,1,64]{2,1,0:T(2,128)(2,1)S(1)} collective-permute-done((bf16[5,1,64]{2,1,0:T(2,128)(2,1)S(1)}, bf16[5,1,64]{2,1,0:T(2,128)(2,1)S(1)}, u32[]{:S(2)}, u32[]{:S(2)}) %collective-permute-start.4) | collective-permute-done | bytes 672 | tf_op jit(solution)/shard_map/ppermute | solution.py:33
  65.2 3.4 %collective-permute-start.5 = (bf16[5,34,1]{2,1,0:T(8,128)(2,1)S(1)}, bf16[5,34,1]{2,1,0:T(8,128)(2,1)S(1)}, u32[]{:S(2)}, u32[]{:S(2)}) collective-permute-start(bf16[5,34,1]{2,1,0:T(8,128)(2,1)S(1)} %get-tuple-element.147), channel_id=1, source_target_pairs={{0,1},{1,2},{2,3},{4,5},{5,6},{6,7},{8,9},{9,10},{10,11},{12,13},{... | collective-permute-start | bytes 1028 | tf_op jit(solution)/shard_map/ppermute | solution.py:31
  68.6 1.9 %collective-permute-start.6 = (bf16[5,34,1]{2,1,0:T(8,128)(2,1)S(1)}, bf16[5,34,1]{2,1,0:T(8,128)(2,1)S(1)}, u32[]{:S(2)}, u32[]{:S(2)}) collective-permute-start(bf16[5,34,1]{2,1,0:T(8,128)(2,1)S(1)} %get-tuple-element.148), channel_id=1, source_target_pairs={{1,0},{2,1},{3,2},{5,4},{6,5},{7,6},{9,8},{10,9},{11,10},{13,12},{... | collective-permute-start | bytes 1028 | tf_op jit(solution)/shard_map/ppermute | solution.py:33
  71.0 3.1 %collective-permute-done.6 = bf16[5,34,1]{2,1,0:T(8,128)(2,1)S(1)} collective-permute-done((bf16[5,34,1]{2,1,0:T(8,128)(2,1)S(1)}, bf16[5,34,1]{2,1,0:T(8,128)(2,1)S(1)}, u32[]{:S(2)}, u32[]{:S(2)}) %collective-permute-start.6) | collective-permute-done | bytes 372 | tf_op jit(solution)/shard_map/ppermute | solution.py:33
  77.2 3.2 %collective-permute-start.7 = (bf16[64,1,64]{0,2,1:T(8,128)(2,1)S(1)}, bf16[64,1,64]{0,2,1:T(8,128)(2,1)S(1)}, u32[]{:S(2)}, u32[]{:S(2)}) collective-permute-start(bf16[64,1,64]{0,2,1:T(8,128)(2,1)S(1)} %get-tuple-element.139), channel_id=1, source_target_pairs={{0,4},{4,8},{8,12},{1,5},{5,9},{9,13},{2,6},{6,10},{10,14},{3,7},{... | collective-permute-start | bytes 24584 | tf_op jit(solution)/shard_map/ppermute | solution.py:31
  82.0 2.9 %collective-permute-done.8 = bf16[64,1,64]{0,2,1:T(8,128)(2,1)S(1)} collective-permute-done((bf16[64,1,64]{0,2,1:T(8,128)(2,1)S(1)}, bf16[64,1,64]{0,2,1:T(8,128)(2,1)S(1)}, u32[]{:S(2)}, u32[]{:S(2)}) %collective-permute-start.8) | collective-permute-done | bytes 8224 | tf_op jit(solution)/shard_map/ppermute | solution.py:33
  84.9 1.9 %collective-permute-start.10 = (bf16[64,34,1]{0,2,1:T(2,128)(2,1)S(1)}, bf16[64,34,1]{0,2,1:T(2,128)(2,1)S(1)}, u32[]{:S(2)}, u32[]{:S(2)}) collective-permute-start(bf16[64,34,1]{0,2,1:T(2,128)(2,1)S(1)} %get-tuple-element.132), channel_id=1, source_target_pairs={{1,0},{2,1},{3,2},{5,4},{6,5},{7,6},{9,8},{10,9},{11,10},{13,12},{... | collective-permute-start | bytes 13064 | tf_op jit(solution)/shard_map/ppermute | solution.py:33
  86.9 3.6 %collective-permute-start.9 = (bf16[64,34,1]{0,2,1:T(2,128)(2,1)S(1)}, bf16[64,34,1]{0,2,1:T(2,128)(2,1)S(1)}, u32[]{:S(2)}, u32[]{:S(2)}) collective-permute-start(bf16[64,34,1]{0,2,1:T(2,128)(2,1)S(1)} %get-tuple-element.131), channel_id=1, source_target_pairs={{0,1},{1,2},{2,3},{4,5},{5,6},{6,7},{8,9},{9,10},{10,11},{12,13},{... | collective-permute-start | bytes 13064 | tf_op jit(solution)/shard_map/ppermute | solution.py:31
  93.7 3.2 %collective-permute-start.11 = (bf16[64,1,64]{0,2,1:T(8,128)(2,1)S(1)}, bf16[64,1,64]{0,2,1:T(8,128)(2,1)S(1)}, u32[]{:S(2)}, u32[]{:S(2)}) collective-permute-start(bf16[64,1,64]{0,2,1:T(8,128)(2,1)S(1)} %get-tuple-element.137), channel_id=1, source_target_pairs={{0,4},{4,8},{8,12},{1,5},{5,9},{9,13},{2,6},{6,10},{10,14},{3,7},{... | collective-permute-start | bytes 24584 | tf_op jit(solution)/shard_map/ppermute | solution.py:31
  98.7 2.7 %collective-permute-done.12 = bf16[64,1,64]{0,2,1:T(8,128)(2,1)S(1)} collective-permute-done((bf16[64,1,64]{0,2,1:T(8,128)(2,1)S(1)}, bf16[64,1,64]{0,2,1:T(8,128)(2,1)S(1)}, u32[]{:S(2)}, u32[]{:S(2)}) %collective-permute-start.12) | collective-permute-done | bytes 8224 | tf_op jit(solution)/shard_map/ppermute | solution.py:33
  101.5 5.6 %collective-permute-start.13 = (bf16[64,34,1]{0,2,1:T(2,128)(2,1)S(1)}, bf16[64,34,1]{0,2,1:T(2,128)(2,1)S(1)}, u32[]{:S(2)}, u32[]{:S(2)}) collective-permute-start(bf16[64,34,1]{0,2,1:T(2,128)(2,1)S(1)} %get-tuple-element.127), channel_id=1, source_target_pairs={{0,1},{1,2},{2,3},{4,5},{5,6},{6,7},{8,9},{9,10},{10,11},{12,13},{... | collective-permute-start | bytes 13064 | tf_op jit(solution)/shard_map/ppermute | solution.py:31
  107.1 1.9 %collective-permute-start.14 = (bf16[64,34,1]{0,2,1:T(2,128)(2,1)S(1)}, bf16[64,34,1]{0,2,1:T(2,128)(2,1)S(1)}, u32[]{:S(2)}, u32[]{:S(2)}) collective-permute-start(bf16[64,34,1]{0,2,1:T(2,128)(2,1)S(1)} %get-tuple-element.128), channel_id=1, source_target_pairs={{1,0},{2,1},{3,2},{5,4},{6,5},{7,6},{9,8},{10,9},{11,10},{13,12},{... | collective-permute-start | bytes 13064 | tf_op jit(solution)/shard_map/ppermute | solution.py:33
  109.7 2.5 %collective-permute-done.14 = bf16[64,34,1]{0,2,1:T(2,128)(2,1)S(1)} collective-permute-done((bf16[64,34,1]{0,2,1:T(2,128)(2,1)S(1)}, bf16[64,34,1]{0,2,1:T(2,128)(2,1)S(1)}, u32[]{:S(2)}, u32[]{:S(2)}) %collective-permute-start.14) | collective-permute-done | bytes 4384 | tf_op jit(solution)/shard_map/ppermute | solution.py:33
  114.7 1.9 %collective-permute-start.15 = (bf16[64,1,64]{0,2,1:T(8,128)(2,1)S(1)}, bf16[64,1,64]{0,2,1:T(8,128)(2,1)S(1)}, u32[]{:S(2)}, u32[]{:S(2)}) collective-permute-start(bf16[64,1,64]{0,2,1:T(8,128)(2,1)S(1)} %get-tuple-element.135), channel_id=1, source_target_pairs={{0,4},{4,8},{8,12},{1,5},{5,9},{9,13},{2,6},{6,10},{10,14},{3,7},{... | collective-permute-start | bytes 24584 | tf_op jit(solution)/shard_map/ppermute | solution.py:31
  118.2 2.9 %collective-permute-done.16 = bf16[64,1,64]{0,2,1:T(8,128)(2,1)S(1)} collective-permute-done((bf16[64,1,64]{0,2,1:T(8,128)(2,1)S(1)}, bf16[64,1,64]{0,2,1:T(8,128)(2,1)S(1)}, u32[]{:S(2)}, u32[]{:S(2)}) %collective-permute-start.16) | collective-permute-done | bytes 8224 | tf_op jit(solution)/shard_map/ppermute | solution.py:33
  121.1 3.4 %collective-permute-start.17 = (bf16[64,34,1]{0,2,1:T(2,128)(2,1)S(1)}, bf16[64,34,1]{0,2,1:T(2,128)(2,1)S(1)}, u32[]{:S(2)}, u32[]{:S(2)}) collective-permute-start(bf16[64,34,1]{0,2,1:T(2,128)(2,1)S(1)} %get-tuple-element.123), channel_id=1, source_target_pairs={{0,1},{1,2},{2,3},{4,5},{5,6},{6,7},{8,9},{9,10},{10,11},{12,13},{... | collective-permute-start | bytes 13064 | tf_op jit(solution)/shard_map/ppermute | solution.py:31
  124.5 1.9 %collective-permute-start.18 = (bf16[64,34,1]{0,2,1:T(2,128)(2,1)S(1)}, bf16[64,34,1]{0,2,1:T(2,128)(2,1)S(1)}, u32[]{:S(2)}, u32[]{:S(2)}) collective-permute-start(bf16[64,34,1]{0,2,1:T(2,128)(2,1)S(1)} %get-tuple-element.124), channel_id=1, source_target_pairs={{1,0},{2,1},{3,2},{5,4},{6,5},{7,6},{9,8},{10,9},{11,10},{13,12},{... | collective-permute-start | bytes 13064 | tf_op jit(solution)/shard_map/ppermute | solution.py:33
  127.0 2.5 %collective-permute-done.18 = bf16[64,34,1]{0,2,1:T(2,128)(2,1)S(1)} collective-permute-done((bf16[64,34,1]{0,2,1:T(2,128)(2,1)S(1)}, bf16[64,34,1]{0,2,1:T(2,128)(2,1)S(1)}, u32[]{:S(2)}, u32[]{:S(2)}) %collective-permute-start.18) | collective-permute-done | bytes 4384 | tf_op jit(solution)/shard_map/ppermute | solution.py:33
  132.0 1.7 %collective-permute-start.19 = (bf16[64,1,64]{0,2,1:T(8,128)(2,1)S(1)}, bf16[64,1,64]{0,2,1:T(8,128)(2,1)S(1)}, u32[]{:S(2)}, u32[]{:S(2)}) collective-permute-start(bf16[64,1,64]{0,2,1:T(8,128)(2,1)S(1)} %get-tuple-element.133), channel_id=1, source_target_pairs={{0,4},{4,8},{8,12},{1,5},{5,9},{9,13},{2,6},{6,10},{10,14},{3,7},{... | collective-permute-start | bytes 24584 | tf_op jit(solution)/shard_map/ppermute | solution.py:31
  135.4 2.7 %collective-permute-done.20 = bf16[64,1,64]{0,2,1:T(8,128)(2,1)S(1)} collective-permute-done((bf16[64,1,64]{0,2,1:T(8,128)(2,1)S(1)}, bf16[64,1,64]{0,2,1:T(8,128)(2,1)S(1)}, u32[]{:S(2)}, u32[]{:S(2)}) %collective-permute-start.20) | collective-permute-done | bytes 8224 | tf_op jit(solution)/shard_map/ppermute | solution.py:33
  138.1 3.4 %collective-permute-start.21 = (bf16[64,34,1]{0,2,1:T(2,128)(2,1)S(1)}, bf16[64,34,1]{0,2,1:T(2,128)(2,1)S(1)}, u32[]{:S(2)}, u32[]{:S(2)}) collective-permute-start(bf16[64,34,1]{0,2,1:T(2,128)(2,1)S(1)} %get-tuple-element.119), channel_id=1, source_target_pairs={{0,1},{1,2},{2,3},{4,5},{5,6},{6,7},{8,9},{9,10},{10,11},{12,13},{... | collective-permute-start | bytes 13064 | tf_op jit(solution)/shard_map/ppermute | solution.py:31
  141.5 1.9 %collective-permute-start.22 = (bf16[64,34,1]{0,2,1:T(2,128)(2,1)S(1)}, bf16[64,34,1]{0,2,1:T(2,128)(2,1)S(1)}, u32[]{:S(2)}, u32[]{:S(2)}) collective-permute-start(bf16[64,34,1]{0,2,1:T(2,128)(2,1)S(1)} %get-tuple-element.120), channel_id=1, source_target_pairs={{1,0},{2,1},{3,2},{5,4},{6,5},{7,6},{9,8},{10,9},{11,10},{13,12},{... | collective-permute-start | bytes 13064 | tf_op jit(solution)/shard_map/ppermute | solution.py:33
  144.5 2.1 %collective-permute-done.22 = bf16[64,34,1]{0,2,1:T(2,128)(2,1)S(1)} collective-permute-done((bf16[64,34,1]{0,2,1:T(2,128)(2,1)S(1)}, bf16[64,34,1]{0,2,1:T(2,128)(2,1)S(1)}, u32[]{:S(2)}, u32[]{:S(2)}) %collective-permute-start.22) | collective-permute-done | bytes 4384 | tf_op jit(solution)/shard_map/ppermute | solution.py:33
  (193 shorter events, 54.2 us)
Async XLA Ops:
  0.6 16.6 %copy-start = (bf16[128,128]{1,0:T(8,128)(2,1)S(1)}, bf16[128,128]{1,0:T(8,128)(2,1)}, u32[]{:S(2)}) copy-start(bf16[128,128]{1,0:T(8,128)(2,1)} %param.15) | copy-start | bytes 98308
  0.6 12.1 %all-to-all-start = ((bf16[32,64,128]{2,1,0:T(8,128)(2,1)}), bf16[32,64,128]{2,1,0:T(8,128)(2,1)S(1)}, u32[]{:S(2)}, u32[]{:S(2)}) async-start(bf16[32,64,128]{2,1,0:T(8,128)(2,1)} %param.13), calls=%async_computation | async-start | bytes 1048576 | tf_op jit(solution)/shard_map/all_to_all | solution.py:106
  12.7 12.5 %all-to-all-start.1 = ((bf16[32,64,128]{2,1,0:T(8,128)(2,1)}), bf16[32,64,128]{2,1,0:T(8,128)(2,1)S(1)}, u32[]{:S(2)}, u32[]{:S(2)}) async-start(bf16[32,64,128]{2,1,0:T(8,128)(2,1)} %param.12), calls=%async_computation.1 | async-start | bytes 1048576 | tf_op jit(solution)/shard_map/all_to_all | solution.py:105
  17.2 0.8 copy-start.3
  25.6 24.2 %copy-start.4 = (bf16[128,128]{1,0:T(8,128)(2,1)S(1)}, bf16[128,128]{1,0:T(8,128)(2,1)}, u32[]{:S(2)}) copy-start(bf16[128,128]{1,0:T(8,128)(2,1)} %param.17) | copy-start | bytes 98308
  50.2 3.6 %copy-start.2 = (f32[3,32,64]{2,1,0:T(8,128)S(1)}, f32[3,32,64]{2,1,0:T(8,128)}, u32[]{:S(2)}) copy-start(f32[3,32,64]{2,1,0:T(8,128)} %param.14) | copy-start | bytes 73732
  50.3 20.3 %copy-start.5 = (bf16[9,64,5]{1,2,0:T(8,128)(2,1)S(1)}, bf16[9,64,5]{1,2,0:T(8,128)(2,1)}, u32[]{:S(2)}) copy-start(bf16[9,64,5]{1,2,0:T(8,128)(2,1)} %param.19) | copy-start | bytes 17284
  51.4 2.3 %collective-permute-start = (f32[1,2,8,64]{3,0,2,1:T(1,128)S(1)}, f32[1,2,8,64]{3,0,2,1:T(1,128)S(1)}, u32[]{:S(2)}, u32[]{:S(2)}) collective-permute-start(f32[1,2,8,64]{3,0,2,1:T(1,128)S(1)} %get-tuple-element.163), channel_id=1, source_target_pairs={{0,1},{1,2},{2,3},{3,0},{4,5},{5,6},{6,7},{7,4},{8,9},{9,10},{10,1... | collective-permute-start | bytes 12296 | tf_op jit(solution)/shard_map/ppermute | solution.py:133
  52.3 2.7 %collective-permute-start.1 = (f32[1,2,8,64]{3,0,2,1:T(1,128)S(1)}, f32[1,2,8,64]{3,0,2,1:T(1,128)S(1)}, u32[]{:S(2)}, u32[]{:S(2)}) collective-permute-start(f32[1,2,8,64]{3,0,2,1:T(1,128)S(1)} %get-tuple-element.162), channel_id=1, source_target_pairs={{0,2},{1,3},{2,0},{3,1},{4,6},{5,7},{6,4},{7,5},{8,10},{9,11},{10,... | collective-permute-start | bytes 12296 | tf_op jit(solution)/shard_map/ppermute | solution.py:133
  53.7 3.1 %collective-permute-start.2 = (f32[1,2,8,64]{3,0,2,1:T(1,128)S(1)}, f32[1,2,8,64]{3,0,2,1:T(1,128)S(1)}, u32[]{:S(2)}, u32[]{:S(2)}) collective-permute-start(f32[1,2,8,64]{3,0,2,1:T(1,128)S(1)} %get-tuple-element.161), channel_id=1, source_target_pairs={{0,3},{1,0},{2,1},{3,2},{4,7},{5,4},{6,5},{7,6},{8,11},{9,8},{10,9... | collective-permute-start | bytes 12296 | tf_op jit(solution)/shard_map/ppermute | solution.py:133
  56.9 5.2 %collective-permute-start.3 = (bf16[5,1,64]{2,1,0:T(2,128)(2,1)S(1)}, bf16[5,1,64]{2,1,0:T(2,128)(2,1)S(1)}, u32[]{:S(2)}, u32[]{:S(2)}) collective-permute-start(bf16[5,1,64]{2,1,0:T(2,128)(2,1)S(1)} %get-tuple-element.153), channel_id=1, source_target_pairs={{0,4},{4,8},{8,12},{1,5},{5,9},{9,13},{2,6},{6,10},{10,14},{3,7},{... | collective-permute-start | bytes 1928 | tf_op jit(solution)/shard_map/ppermute | solution.py:31
  60.8 4.3 %collective-permute-start.4 = (bf16[5,1,64]{2,1,0:T(2,128)(2,1)S(1)}, bf16[5,1,64]{2,1,0:T(2,128)(2,1)S(1)}, u32[]{:S(2)}, u32[]{:S(2)}) collective-permute-start(bf16[5,1,64]{2,1,0:T(2,128)(2,1)S(1)} %get-tuple-element.154), channel_id=1, source_target_pairs={{4,0},{8,4},{12,8},{5,1},{9,5},{13,9},{6,2},{10,6},{14,10},{7,3},{... | collective-permute-start | bytes 1928 | tf_op jit(solution)/shard_map/ppermute | solution.py:33
  65.2 5.7 %collective-permute-start.5 = (bf16[5,34,1]{2,1,0:T(8,128)(2,1)S(1)}, bf16[5,34,1]{2,1,0:T(8,128)(2,1)S(1)}, u32[]{:S(2)}, u32[]{:S(2)}) collective-permute-start(bf16[5,34,1]{2,1,0:T(8,128)(2,1)S(1)} %get-tuple-element.147), channel_id=1, source_target_pairs={{0,1},{1,2},{2,3},{4,5},{5,6},{6,7},{8,9},{9,10},{10,11},{12,13},{... | collective-permute-start | bytes 1028 | tf_op jit(solution)/shard_map/ppermute | solution.py:31
  68.6 5.4 %collective-permute-start.6 = (bf16[5,34,1]{2,1,0:T(8,128)(2,1)S(1)}, bf16[5,34,1]{2,1,0:T(8,128)(2,1)S(1)}, u32[]{:S(2)}, u32[]{:S(2)}) collective-permute-start(bf16[5,34,1]{2,1,0:T(8,128)(2,1)S(1)} %get-tuple-element.148), channel_id=1, source_target_pairs={{1,0},{2,1},{3,2},{5,4},{6,5},{7,6},{9,8},{10,9},{11,10},{13,12},{... | collective-permute-start | bytes 1028 | tf_op jit(solution)/shard_map/ppermute | solution.py:33
  76.8 4.9 %copy-start.1 = (bf16[3,9,64,64]{3,2,1,0:T(8,128)(2,1)S(1)}, bf16[3,9,64,64]{3,2,1,0:T(8,128)(2,1)}, u32[]{:S(2)}) copy-start(bf16[3,9,64,64]{3,2,1,0:T(8,128)(2,1)} %param.20) | copy-start | bytes 663556
  77.2 4.8 %collective-permute-start.7 = (bf16[64,1,64]{0,2,1:T(8,128)(2,1)S(1)}, bf16[64,1,64]{0,2,1:T(8,128)(2,1)S(1)}, u32[]{:S(2)}, u32[]{:S(2)}) collective-permute-start(bf16[64,1,64]{0,2,1:T(8,128)(2,1)S(1)} %get-tuple-element.139), channel_id=1, source_target_pairs={{0,4},{4,8},{8,12},{1,5},{5,9},{9,13},{2,6},{6,10},{10,14},{3,7},{... | collective-permute-start | bytes 24584 | tf_op jit(solution)/shard_map/ppermute | solution.py:31
  80.4 4.5 %collective-permute-start.8 = (bf16[64,1,64]{0,2,1:T(8,128)(2,1)S(1)}, bf16[64,1,64]{0,2,1:T(8,128)(2,1)S(1)}, u32[]{:S(2)}, u32[]{:S(2)}) collective-permute-start(bf16[64,1,64]{0,2,1:T(8,128)(2,1)S(1)} %get-tuple-element.140), channel_id=1, source_target_pairs={{4,0},{8,4},{12,8},{5,1},{9,5},{13,9},{6,2},{10,6},{14,10},{7,3},{... | collective-permute-start | bytes 24584 | tf_op jit(solution)/shard_map/ppermute | solution.py:33
  84.9 6.2 %collective-permute-start.10 = (bf16[64,34,1]{0,2,1:T(2,128)(2,1)S(1)}, bf16[64,34,1]{0,2,1:T(2,128)(2,1)S(1)}, u32[]{:S(2)}, u32[]{:S(2)}) collective-permute-start(bf16[64,34,1]{0,2,1:T(2,128)(2,1)S(1)} %get-tuple-element.132), channel_id=1, source_target_pairs={{1,0},{2,1},{3,2},{5,4},{6,5},{7,6},{9,8},{10,9},{11,10},{13,12},{... | collective-permute-start | bytes 13064 | tf_op jit(solution)/shard_map/ppermute | solution.py:33
  86.9 4.5 %collective-permute-start.9 = (bf16[64,34,1]{0,2,1:T(2,128)(2,1)S(1)}, bf16[64,34,1]{0,2,1:T(2,128)(2,1)S(1)}, u32[]{:S(2)}, u32[]{:S(2)}) collective-permute-start(bf16[64,34,1]{0,2,1:T(2,128)(2,1)S(1)} %get-tuple-element.131), channel_id=1, source_target_pairs={{0,1},{1,2},{2,3},{4,5},{5,6},{6,7},{8,9},{9,10},{10,11},{12,13},{... | collective-permute-start | bytes 13064 | tf_op jit(solution)/shard_map/ppermute | solution.py:31
  93.7 5.0 %collective-permute-start.11 = (bf16[64,1,64]{0,2,1:T(8,128)(2,1)S(1)}, bf16[64,1,64]{0,2,1:T(8,128)(2,1)S(1)}, u32[]{:S(2)}, u32[]{:S(2)}) collective-permute-start(bf16[64,1,64]{0,2,1:T(8,128)(2,1)S(1)} %get-tuple-element.137), channel_id=1, source_target_pairs={{0,4},{4,8},{8,12},{1,5},{5,9},{9,13},{2,6},{6,10},{10,14},{3,7},{... | collective-permute-start | bytes 24584 | tf_op jit(solution)/shard_map/ppermute | solution.py:31
  97.0 4.5 %collective-permute-start.12 = (bf16[64,1,64]{0,2,1:T(8,128)(2,1)S(1)}, bf16[64,1,64]{0,2,1:T(8,128)(2,1)S(1)}, u32[]{:S(2)}, u32[]{:S(2)}) collective-permute-start(bf16[64,1,64]{0,2,1:T(8,128)(2,1)S(1)} %get-tuple-element.138), channel_id=1, source_target_pairs={{4,0},{8,4},{12,8},{5,1},{9,5},{13,9},{6,2},{10,6},{14,10},{7,3},{... | collective-permute-start | bytes 24584 | tf_op jit(solution)/shard_map/ppermute | solution.py:33
  101.5 8.2 %collective-permute-start.13 = (bf16[64,34,1]{0,2,1:T(2,128)(2,1)S(1)}, bf16[64,34,1]{0,2,1:T(2,128)(2,1)S(1)}, u32[]{:S(2)}, u32[]{:S(2)}) collective-permute-start(bf16[64,34,1]{0,2,1:T(2,128)(2,1)S(1)} %get-tuple-element.127), channel_id=1, source_target_pairs={{0,1},{1,2},{2,3},{4,5},{5,6},{6,7},{8,9},{9,10},{10,11},{12,13},{... | collective-permute-start | bytes 13064 | tf_op jit(solution)/shard_map/ppermute | solution.py:31
  107.1 5.1 %collective-permute-start.14 = (bf16[64,34,1]{0,2,1:T(2,128)(2,1)S(1)}, bf16[64,34,1]{0,2,1:T(2,128)(2,1)S(1)}, u32[]{:S(2)}, u32[]{:S(2)}) collective-permute-start(bf16[64,34,1]{0,2,1:T(2,128)(2,1)S(1)} %get-tuple-element.128), channel_id=1, source_target_pairs={{1,0},{2,1},{3,2},{5,4},{6,5},{7,6},{9,8},{10,9},{11,10},{13,12},{... | collective-permute-start | bytes 13064 | tf_op jit(solution)/shard_map/ppermute | solution.py:33
  114.7 3.5 %collective-permute-start.15 = (bf16[64,1,64]{0,2,1:T(8,128)(2,1)S(1)}, bf16[64,1,64]{0,2,1:T(8,128)(2,1)S(1)}, u32[]{:S(2)}, u32[]{:S(2)}) collective-permute-start(bf16[64,1,64]{0,2,1:T(8,128)(2,1)S(1)} %get-tuple-element.135), channel_id=1, source_target_pairs={{0,4},{4,8},{8,12},{1,5},{5,9},{9,13},{2,6},{6,10},{10,14},{3,7},{... | collective-permute-start | bytes 24584 | tf_op jit(solution)/shard_map/ppermute | solution.py:31
  116.6 4.5 %collective-permute-start.16 = (bf16[64,1,64]{0,2,1:T(8,128)(2,1)S(1)}, bf16[64,1,64]{0,2,1:T(8,128)(2,1)S(1)}, u32[]{:S(2)}, u32[]{:S(2)}) collective-permute-start(bf16[64,1,64]{0,2,1:T(8,128)(2,1)S(1)} %get-tuple-element.136), channel_id=1, source_target_pairs={{4,0},{8,4},{12,8},{5,1},{9,5},{13,9},{6,2},{10,6},{14,10},{7,3},{... | collective-permute-start | bytes 24584 | tf_op jit(solution)/shard_map/ppermute | solution.py:33
  121.1 5.9 %collective-permute-start.17 = (bf16[64,34,1]{0,2,1:T(2,128)(2,1)S(1)}, bf16[64,34,1]{0,2,1:T(2,128)(2,1)S(1)}, u32[]{:S(2)}, u32[]{:S(2)}) collective-permute-start(bf16[64,34,1]{0,2,1:T(2,128)(2,1)S(1)} %get-tuple-element.123), channel_id=1, source_target_pairs={{0,1},{1,2},{2,3},{4,5},{5,6},{6,7},{8,9},{9,10},{10,11},{12,13},{... | collective-permute-start | bytes 13064 | tf_op jit(solution)/shard_map/ppermute | solution.py:31
  124.5 5.1 %collective-permute-start.18 = (bf16[64,34,1]{0,2,1:T(2,128)(2,1)S(1)}, bf16[64,34,1]{0,2,1:T(2,128)(2,1)S(1)}, u32[]{:S(2)}, u32[]{:S(2)}) collective-permute-start(bf16[64,34,1]{0,2,1:T(2,128)(2,1)S(1)} %get-tuple-element.124), channel_id=1, source_target_pairs={{1,0},{2,1},{3,2},{5,4},{6,5},{7,6},{9,8},{10,9},{11,10},{13,12},{... | collective-permute-start | bytes 13064 | tf_op jit(solution)/shard_map/ppermute | solution.py:33
  131.5 3.4 %copy-start.7 = (bf16[9,2,64]{2,1,0:T(2,128)(2,1)S(1)}, bf16[9,2,64]{2,1,0:T(2,128)(2,1)}, u32[]{:S(2)}) copy-start(bf16[9,2,64]{2,1,0:T(2,128)(2,1)} %param.21) | copy-start | bytes 6916
  132.0 3.5 %collective-permute-start.19 = (bf16[64,1,64]{0,2,1:T(8,128)(2,1)S(1)}, bf16[64,1,64]{0,2,1:T(8,128)(2,1)S(1)}, u32[]{:S(2)}, u32[]{:S(2)}) collective-permute-start(bf16[64,1,64]{0,2,1:T(8,128)(2,1)S(1)} %get-tuple-element.133), channel_id=1, source_target_pairs={{0,4},{4,8},{8,12},{1,5},{5,9},{9,13},{2,6},{6,10},{10,14},{3,7},{... | collective-permute-start | bytes 24584 | tf_op jit(solution)/shard_map/ppermute | solution.py:31
  133.6 4.5 %collective-permute-start.20 = (bf16[64,1,64]{0,2,1:T(8,128)(2,1)S(1)}, bf16[64,1,64]{0,2,1:T(8,128)(2,1)S(1)}, u32[]{:S(2)}, u32[]{:S(2)}) collective-permute-start(bf16[64,1,64]{0,2,1:T(8,128)(2,1)S(1)} %get-tuple-element.134), channel_id=1, source_target_pairs={{4,0},{8,4},{12,8},{5,1},{9,5},{13,9},{6,2},{10,6},{14,10},{7,3},{... | collective-permute-start | bytes 24584 | tf_op jit(solution)/shard_map/ppermute | solution.py:33
  138.1 6.3 %collective-permute-start.21 = (bf16[64,34,1]{0,2,1:T(2,128)(2,1)S(1)}, bf16[64,34,1]{0,2,1:T(2,128)(2,1)S(1)}, u32[]{:S(2)}, u32[]{:S(2)}) collective-permute-start(bf16[64,34,1]{0,2,1:T(2,128)(2,1)S(1)} %get-tuple-element.119), channel_id=1, source_target_pairs={{0,1},{1,2},{2,3},{4,5},{5,6},{6,7},{8,9},{9,10},{10,11},{12,13},{... | collective-permute-start | bytes 13064 | tf_op jit(solution)/shard_map/ppermute | solution.py:31
  141.5 5.1 %collective-permute-start.22 = (bf16[64,34,1]{0,2,1:T(2,128)(2,1)S(1)}, bf16[64,34,1]{0,2,1:T(2,128)(2,1)S(1)}, u32[]{:S(2)}, u32[]{:S(2)}) collective-permute-start(bf16[64,34,1]{0,2,1:T(2,128)(2,1)S(1)} %get-tuple-element.120), channel_id=1, source_target_pairs={{1,0},{2,1},{3,2},{5,4},{6,5},{7,6},{9,8},{10,9},{11,10},{13,12},{... | collective-permute-start | bytes 13064 | tf_op jit(solution)/shard_map/ppermute | solution.py:33
  (1 other events, 0.7 us)
